TPU v7x, 32 devices: a whole 2x2x4 slice. The times are simulated.
32 devices in a mesh: row: 8 (over z, x), col: 4 (over y, core).
Axes of the slice: x: 2, y: 2, z: 4, core: 2. Of those that a mesh axis runs over, the one named last changes fastest.
Arguments:
- vectors: float32 [8, 4096], P(None, ('row', 'col')), may hold values from -6 to 6
- values: float32 [512, 16384], P('row', 'col'), may hold values from -1 to 1
- block_rows: int32 [8, 256], P('row', 'col'), may hold values from 0 to 7
- block_cols: int32 [8, 256], P('row', 'col'), may hold values from 0 to 15
- counts: int32 [8, 4], P('row', 'col'), may hold values from 16 to 64, as said below
Outputs:
- product: float32 [8, 4096], P(None, ('row', 'col'))
Inputs may be any that keep to these rules, and one draw needn't show every extreme that they name: counts[r, c] slots of tile (r, c) hold blocks, the others are unused; some tile uses all 64 slots.
All inputs are finite; a program needn't handle non-finite values.
Results may differ from a plain program's by a relative error of at most 0.0003.
Values sent between devices are 32-bit elements; how exact they have to be, the bound alone decides.
No kernel may reach another device: no remote copies, remote signals or barrier semaphores. Data moves between devices by JAX's collectives and lax.ppermute only.
A program may use at most 64 MiB of HBM per device.

v0:
```python
import jax
import jax.numpy as jnp
from jax import lax
from jax.sharding import PartitionSpec as P

BLK = 64


def tile_terms(blocks, rows, cols, count, row_seg, col_seg):
    highest = lax.Precision.HIGHEST
    slots = blocks.shape[0]
    nvec = row_seg.shape[0]
    row_blocks = row_seg.shape[1] // blocks.shape[1]
    col_blocks = col_seg.shape[1] // blocks.shape[1]
    width = blocks.shape[1]
    live = (jnp.arange(slots, dtype=jnp.int32) < count).astype(jnp.float32)
    row_hits = (rows[:, None] == jnp.arange(row_blocks, dtype=jnp.int32)[None, :]).astype(
        jnp.float32
    ) * live[:, None]
    col_hits = (cols[:, None] == jnp.arange(col_blocks, dtype=jnp.int32)[None, :]).astype(
        jnp.float32
    ) * live[:, None]
    row_parts = row_seg.reshape(nvec, row_blocks, width)
    col_parts = col_seg.reshape(nvec, col_blocks, width)
    col_pick = jnp.take(col_parts, cols, axis=1)
    row_pick = jnp.take(row_parts, rows, axis=1)
    plain = jnp.einsum("kij,vkj->vki", blocks, col_pick, precision=highest)
    turned = jnp.einsum("kji,vkj->vki", blocks, row_pick, precision=highest)
    plain_part = jnp.einsum("kb,vki->vbi", row_hits, plain, precision=highest).reshape(
        nvec, row_blocks * width
    )
    turned_part = jnp.einsum("kb,vki->vbi", col_hits, turned, precision=highest).reshape(
        nvec, col_blocks * width
    )
    return (plain_part, turned_part)


def sum_rows(plain_part):
    return lax.psum_scatter(plain_part, "col", scatter_dimension=1, tiled=True)


def sum_columns(turned_part):
    return lax.psum_scatter(turned_part, "row", scatter_dimension=1, tiled=True)


def per_device(vectors, values, block_rows, block_cols, counts):
    row_seg = lax.all_gather(vectors, "col", axis=1, tiled=True)
    col_seg = lax.all_gather(vectors, "row", axis=1, tiled=True)
    blocks = values.reshape(values.shape[0], BLK, BLK)
    rows = block_rows[0]
    cols = block_cols[0]
    count = counts[0, 0]
    plain_part, turned_part = tile_terms(blocks, rows, cols, count, row_seg, col_seg)
    plain_sum = sum_rows(plain_part)
    turned_sum = sum_columns(turned_part)
    return plain_sum + turned_sum


def solution(mesh):
    in_specs = (
        P(None, ("row", "col")),
        P("row", "col"),
        P("row", "col"),
        P("row", "col"),
        P("row", "col"),
    )
    out_specs = P(None, ("row", "col"))
    return jax.shard_map(
        per_device, mesh=mesh, in_specs=in_specs, out_specs=out_specs, check_vma=False
    )
```

profile of v0, /device:TPU:0, one launch (start us, length us, event | category | flops | bytes accessed | tf_op | source)
XLA Modules:
  0.0 134.8 jit_solution(16836529348863672988)
XLA Ops:
  6.5 0.0 copy-start
  6.5 0.0 reduce-scatter.3.cloned.1.call-start
  6.5 0.7 fusion.20
  7.2 0.7 compare_and_fusion.1
  7.9 2.0 %reshape.91 = f32[64,64,64]{2,1,0:T(8,128)S(1)} reshape(f32[64,4096]{1,0:T(8,128)} %param.6) | data formatting | bytes 2097152 | tf_op jit(solution)/shard_map/reshape | solution.py:49
  9.9 0.0 copy-done
  9.9 0.0 copy-start.1
  9.9 32.4 %all_gather.6 = f32[8,1024]{1,0:T(8,128)S(1)} all-gather(f32[8,128]{1,0:T(8,128)S(1)} %copy-done), channel_id=1, replica_groups=mesh['row'=8,'col'=4] {'row'}, dimensions={1}, use_global_device_ids=true | all-gather | bytes 36864 | tf_op jit(solution)/shard_map/all_gather | solution.py:48
  42.3 0.1 reshape.90
  43.1 0.6 gather_fusion
  43.7 3.4 %convolution_bitcast_fusion.1 = f32[8,64,64]{2,0,1:T(8,128)S(1)} fusion(f32[64,64,64]{2,1,0:T(8,128)S(1)} %reshape.91, f32[64,8,64]{2,1,0:T(8,128)S(1)} %gather_fusion, pred[64]{0:T(512)(128)(4,1)S(1)} %compare_and_fusion.1), kind=kOutput, calls=%fused_computation.3 | convolution fusion | flops 25198592 | bytes 1310784 | tf_op jit(solution)/shard_map/kij,vkj->vki/dot_general | solution.py:27
  47.1 0.0 copy-start.2
  47.2 0.0 copy-done.1
  47.2 0.3 convolution_bitcast_fusion.3
  47.4 0.7 reshape.92
  48.1 0.0 reduce-scatter.3.cloned.1.call-update
  48.1 0.0 reduce-scatter.5.cloned.1.call-start
  48.2 5.2 %all_gather.7 = f32[8,512]{1,0:T(8,128)S(1)} all-gather(f32[8,128]{1,0:T(8,128)S(1)} %copy-done), channel_id=1, replica_groups=mesh['row'=8,'col'=4] {'col'}, dimensions={1}, use_global_device_ids=true | all-gather | bytes 20480 | tf_op jit(solution)/shard_map/all_gather | solution.py:47
  53.4 0.1 reshape.93
  53.5 0.6 gather_fusion.1
  54.1 1.9 %convolution_bitcast_fusion = f32[8,64,64]{2,0,1:T(8,128)S(1)} fusion(f32[64,64,64]{2,1,0:T(8,128)S(1)} %reshape.91, f32[64,8,64]{2,1,0:T(8,128)S(1)} %gather_fusion.1, pred[64]{0:T(512)(128)(4,1)S(1)} %compare_and_fusion), kind=kOutput, calls=%fused_computation.2 | convolution fusion | flops 25198592 | bytes 1310784 | tf_op jit(solution)/shard_map/kji,vkj->vki/dot_general | solution.py:28
  56.1 0.0 copy-done.2
  56.1 0.3 convolution_bitcast_fusion.2
  56.3 0.7 reshape.94
  57.0 0.0 reduce-scatter.5.cloned.1.call-update
  57.0 11.7 %reduce-scatter.3.cloned.1.call-done = f32[8,128]{1,0:T(8,128)} async-done(((f32[8,512]{1,0:T(8,128)}), f32[8,128]{1,0:T(8,128)}) %reduce-scatter.3.cloned.1.call-update) | async-done | bytes 4112 | tf_op jit(solution)/shard_map/reduce_scatter | solution.py:39
  68.7 57.9 %reduce-scatter.5.cloned.1.call-done = f32[8,128]{1,0:T(8,128)} async-done(((f32[8,1024]{1,0:T(8,128)}), f32[8,128]{1,0:T(8,128)}) %reduce-scatter.5.cloned.1.call-update) | async-done | bytes 4112 | tf_op jit(solution)/shard_map/reduce_scatter | solution.py:43
  126.6 1.3 add.57
  (7 shorter events, 0.1 us)
Async XLA Ops:
  6.5 3.3 %copy-start = (f32[8,128]{1,0:T(8,128)S(1)}, f32[8,128]{1,0:T(8,128)}, u32[]{:S(2)}) copy-start(f32[8,128]{1,0:T(8,128)} %param.5) | copy-start | bytes 12292
  6.5 62.2 %reduce-scatter.3.cloned.1.call-start = ((), (), s32[]{:S(2)}) async-start(), calls=%async_computation.2 | async-start | bytes 20480 | tf_op jit(solution)/shard_map/reduce_scatter | solution.py:39
  9.9 37.3 %copy-start.1 = (s32[1,64]{1,0:T(1,128)S(1)}, s32[1,64]{1,0:T(1,128)}, u32[]{:S(2)}) copy-start(s32[1,64]{1,0:T(1,128)} %param.7) | copy-start | bytes 772
  47.1 8.9 %copy-start.2 = (s32[1,64]{1,0:T(1,128)S(1)}, s32[1,64]{1,0:T(1,128)}, u32[]{:S(2)}) copy-start(s32[1,64]{1,0:T(1,128)} %param.8) | copy-start | bytes 772
  48.1 78.5 %reduce-scatter.5.cloned.1.call-start = ((), (), s32[]{:S(2)}) async-start(), calls=%async_computation.3 | async-start | bytes 36864 | tf_op jit(solution)/shard_map/reduce_scatter | solution.py:43
Sparse Core Ops, SparseCore 0:
  48.3 20.4 reduce-scatter.2
  71.9 54.7 reduce-scatter.4
where the time goes:
time: 135 us
  waiting for transfers between devices  69.6 us (52%)
  blocking collectives  37.6 us (28%)
  between operations  14.1 us (10%)
  matrix products  5.88 us (4%)
  local copies, waits for them, and re-layouts  4.82 us (4%)
  other arithmetic  2.63 us (2%)
    reduce_scatter x1, waiting for transfers between devices, sum_columns(): return lax.psum_scatter(turned_part, 'row', scatter_dimension=1, tiled=True)  57.9 us
    all_gather x1, blocking collectives, per_device(): col_seg = lax.all_gather(vectors, 'row', axis=1, tiled=True)  32.4 us
    reduce_scatter x1, waiting for transfers between devices, sum_rows(): return lax.psum_scatter(plain_part, 'col', scatter_dimension=1, tiled=True)  11.7 us
    all_gather x1, blocking collectives, per_device(): row_seg = lax.all_gather(vectors, 'col', axis=1, tiled=True)  5.21 us
    dot_general x1, matrix products, tile_terms(): plain = jnp.einsum('kij,vkj->vki', blocks, col_pick, precision=highest)  3.41 us
  transfers between devices with their start and end apart: 2, of which 2 were waited for; matrix products, arithmetic and copies ran while one was open for 3% of the time, Pallas kernels for 0%

commit v1 on v0

--- a/solution.py
+++ b/solution.py
@@ -4,6 +4,17 @@
 from jax.sharding import PartitionSpec as P
 
 BLK = 64
+
+
+def turned_line(x, mesh_axis, dim):
+    size = lax.axis_size(mesh_axis)
+    right = [(i, (i + 1) % size) for i in range(size)]
+    parts = [x]
+    for far in range(1, size):
+        parts = [lax.ppermute(parts[0], mesh_axis, right), *parts]
+    out = jnp.concatenate(parts, axis=dim)
+    shift = (lax.axis_index(mesh_axis) + 1) * parts[-1].shape[dim]
+    return jnp.roll(out, shift, axis=dim)
 
 
 def tile_terms(blocks, rows, cols, count, row_seg, col_seg):
@@ -45,7 +56,7 @@
 
 def per_device(vectors, values, block_rows, block_cols, counts):
     row_seg = lax.all_gather(vectors, "col", axis=1, tiled=True)
-    col_seg = lax.all_gather(vectors, "row", axis=1, tiled=True)
+    col_seg = turned_line(vectors, "row", 1)
     blocks = values.reshape(values.shape[0], BLK, BLK)
     rows = block_rows[0]
     cols = block_cols[0]

time: 135 us -> 141 us (1.044)
  waiting for transfers between devices: 69.6 us -> 104 us
  blocking collectives: 37.6 us -> 5.19 us
  starting transfers between devices: 0.04 us -> 4.31 us
    all_gather x1 -> x0, blocking collectives: 32.4 us -> none  [per_device(): col_seg = lax.all_gather(vectors, 'row', axis=1, tiled=True)]
    ppermute x0 -> x7, waiting for transfers between devices: none -> 29.5 us  [turned_line(): parts = [lax.ppermute(parts[0], mesh_axis, right), *parts]]
    reduce_scatter x1, waiting for transfers between devices: 11.7 us -> 16.1 us  [sum_rows(): return lax.psum_scatter(plain_part, 'col', scatter_dimension=1, tiled=True)]
    ppermute x0 -> x7, starting transfers between devices: none -> 4.27 us  [turned_line(): parts = [lax.ppermute(parts[0], mesh_axis, right), *parts]]
  transfers between devices with their start and end apart: 2 -> 9, of which waited for: 2 -> 9; matrix products, arithmetic and copies ran while one was open for 3% -> 5% of each run, Pallas kernels for 0% -> 0%
where the time goes in v1:
time: 141 us
  waiting for transfers between devices  104 us (74%)
  between operations  14.2 us (10%)
  matrix products  5.89 us (4%)
  blocking collectives  5.19 us (4%)
  local copies, waits for them, and re-layouts  4.89 us (3%)
  starting transfers between devices  4.31 us (3%)
  other arithmetic  2.62 us (2%)
    reduce_scatter x1, waiting for transfers between devices, sum_columns(): return lax.psum_scatter(turned_part, 'row', scatter_dimension=1, tiled=True)  57.9 us
    ppermute x7, waiting for transfers between devices, turned_line(): parts = [lax.ppermute(parts[0], mesh_axis, right), *parts]  29.5 us
    reduce_scatter x1, waiting for transfers between devices, sum_rows(): return lax.psum_scatter(plain_part, 'col', scatter_dimension=1, tiled=True)  16.1 us
    all_gather x1, blocking collectives, per_device(): row_seg = lax.all_gather(vectors, 'col', axis=1, tiled=True)  5.19 us
    ppermute x7, starting transfers between devices, turned_line(): parts = [lax.ppermute(parts[0], mesh_axis, right), *parts]  4.27 us
    dot_general x1, matrix products, tile_terms(): plain = jnp.einsum('kij,vkj->vki', blocks, col_pick, precision=highest)  3.41 us
  transfers between devices with their start and end apart: 9, of which 9 were waited for; matrix products, arithmetic and copies ran while one was open for 5% of the time, Pallas kernels for 0%

profile of v1, /device:TPU:0, one launch (start us, length us, event | category | flops | bytes accessed | tf_op | source)
XLA Modules:
  0.0 140.6 jit_solution(4016944540735201439)
XLA Ops:
  6.5 0.0 copy-start
  6.5 0.0 reduce-scatter.3.cloned.1.call-start
  6.5 3.0 %collective-permute-start = (f32[8,128]{1,0:T(8,128)}, f32[8,128]{1,0:T(8,128)S(1)}, u32[]{:S(2)}, u32[]{:S(2)}) collective-permute-start(f32[8,128]{1,0:T(8,128)} %param.5), channel_id=1, source_target_pairs={{0,4},{4,8},{8,12},{12,16},{16,20},{20,24},{24,28},{28,0},{1,5},{5... | collective-permute-start | bytes 12296 | tf_op jit(solution)/shard_map/ppermute | solution.py:14
  9.5 0.7 fusion.21
  10.2 0.7 compare_and_fusion
  10.8 2.0 %reshape.91 = f32[64,64,64]{2,1,0:T(8,128)S(1)} reshape(f32[64,4096]{1,0:T(8,128)} %param.6) | data formatting | bytes 2097152 | tf_op jit(solution)/shard_map/reshape | solution.py:60
  12.8 0.0 copy-start.2
  12.9 1.5 %collective-permute-done = f32[8,128]{1,0:T(8,128)S(1)} collective-permute-done((f32[8,128]{1,0:T(8,128)}, f32[8,128]{1,0:T(8,128)S(1)}, u32[]{:S(2)}, u32[]{:S(2)}) %collective-permute-start) | collective-permute-done | bytes 4128 | tf_op jit(solution)/shard_map/ppermute | solution.py:14
  14.4 0.1 collective-permute-start.1
  14.5 0.0 copy-done
  14.5 5.2 %all_gather.3 = f32[8,512]{1,0:T(8,128)S(1)} all-gather(f32[8,128]{1,0:T(8,128)S(1)} %copy-done), channel_id=1, replica_groups=mesh['row'=8,'col'=4] {'col'}, dimensions={1}, use_global_device_ids=true | all-gather | bytes 20480 | tf_op jit(solution)/shard_map/all_gather | solution.py:58
  19.7 0.1 reshape.93
  19.7 0.6 gather_fusion.1
  20.4 0.3 collective-permute-done.1
  20.7 1.2 collective-permute-start.2
  21.9 1.9 %convolution_bitcast_fusion = f32[8,64,64]{2,0,1:T(8,128)S(1)} fusion(f32[64,64,64]{2,1,0:T(8,128)S(1)} %reshape.91, f32[64,8,64]{2,1,0:T(8,128)S(1)} %gather_fusion.1, pred[64]{0:T(512)(128)(4,1)S(1)} %compare_and_fusion), kind=kOutput, calls=%fused_computation.2 | convolution fusion | flops 25198592 | bytes 1310784 | tf_op jit(solution)/shard_map/kji,vkj->vki/dot_general | solution.py:39
  23.9 0.0 copy-start.1
  23.9 3.1 %collective-permute-done.2 = f32[8,128]{1,0:T(8,128)S(1)} collective-permute-done((f32[8,128]{1,0:T(8,128)S(1)}, f32[8,128]{1,0:T(8,128)S(1)}, u32[]{:S(2)}, u32[]{:S(2)}) %collective-permute-start.2) | collective-permute-done | bytes 4128 | tf_op jit(solution)/shard_map/ppermute | solution.py:14
  27.0 0.0 collective-permute-start.3
  27.0 0.0 copy-done.2
  27.0 6.3 %collective-permute-done.3 = f32[8,128]{1,0:T(8,128)S(1)} collective-permute-done((f32[8,128]{1,0:T(8,128)S(1)}, f32[8,128]{1,0:T(8,128)S(1)}, u32[]{:S(2)}, u32[]{:S(2)}) %collective-permute-start.3) | collective-permute-done | bytes 4128 | tf_op jit(solution)/shard_map/ppermute | solution.py:14
  33.3 0.0 collective-permute-start.4
  33.3 6.3 %collective-permute-done.4 = f32[8,128]{1,0:T(8,128)S(1)} collective-permute-done((f32[8,128]{1,0:T(8,128)S(1)}, f32[8,128]{1,0:T(8,128)S(1)}, u32[]{:S(2)}, u32[]{:S(2)}) %collective-permute-start.4) | collective-permute-done | bytes 4128 | tf_op jit(solution)/shard_map/ppermute | solution.py:14
  39.6 0.0 collective-permute-start.5
  40.3 5.6 %collective-permute-done.5 = f32[8,128]{1,0:T(8,128)S(1)} collective-permute-done((f32[8,128]{1,0:T(8,128)S(1)}, f32[8,128]{1,0:T(8,128)S(1)}, u32[]{:S(2)}, u32[]{:S(2)}) %collective-permute-start.5) | collective-permute-done | bytes 4128 | tf_op jit(solution)/shard_map/ppermute | solution.py:14
  45.9 0.0 collective-permute-start.6
  45.9 6.3 %collective-permute-done.6 = f32[8,128]{1,0:T(8,128)S(1)} collective-permute-done((f32[8,128]{1,0:T(8,128)S(1)}, f32[8,128]{1,0:T(8,128)S(1)}, u32[]{:S(2)}, u32[]{:S(2)}) %collective-permute-start.6) | collective-permute-done | bytes 4128 | tf_op jit(solution)/shard_map/ppermute | solution.py:14
  52.4 0.1 reshape.90
  52.5 0.6 gather_fusion
  53.1 3.4 %convolution_bitcast_fusion.1 = f32[8,64,64]{2,0,1:T(8,128)S(1)} fusion(f32[64,64,64]{2,1,0:T(8,128)S(1)} %reshape.91, f32[64,8,64]{2,1,0:T(8,128)S(1)} %gather_fusion, pred[64]{0:T(512)(128)(4,1)S(1)} %compare_and_fusion.1), kind=kOutput, calls=%fused_computation.3 | convolution fusion | flops 25198592 | bytes 1310784 | tf_op jit(solution)/shard_map/kij,vkj->vki/dot_general | solution.py:38
  56.6 0.0 copy-done.1
  56.6 0.3 convolution_bitcast_fusion.3
  56.8 0.7 reshape.92
  57.5 0.0 reduce-scatter.3.cloned.1.call-update
  57.5 0.0 reduce-scatter.5.cloned.1.call-start
  57.6 0.3 convolution_bitcast_fusion.2
  57.9 0.7 reshape.94
  58.6 0.0 reduce-scatter.5.cloned.1.call-update
  58.6 16.1 %reduce-scatter.3.cloned.1.call-done = f32[8,128]{1,0:T(8,128)} async-done(((f32[8,512]{1,0:T(8,128)}), f32[8,128]{1,0:T(8,128)}) %reduce-scatter.3.cloned.1.call-update) | async-done | bytes 4112 | tf_op jit(solution)/shard_map/reduce_scatter | solution.py:50
  74.7 57.9 %reduce-scatter.5.cloned.1.call-done = f32[8,128]{1,0:T(8,128)} async-done(((f32[8,1024]{1,0:T(8,128)}), f32[8,128]{1,0:T(8,128)}) %reduce-scatter.5.cloned.1.call-update) | async-done | bytes 4112 | tf_op jit(solution)/shard_map/reduce_scatter | solution.py:54
  132.5 1.3 add.73
  (24 shorter events, 0.1 us)
Async XLA Ops:
  6.5 7.9 %copy-start = (f32[8,128]{1,0:T(8,128)S(1)}, f32[8,128]{1,0:T(8,128)}, u32[]{:S(2)}) copy-start(f32[8,128]{1,0:T(8,128)} %param.5) | copy-start | bytes 12292
  6.5 68.1 %reduce-scatter.3.cloned.1.call-start = ((), (), s32[]{:S(2)}) async-start(), calls=%async_computation.2 | async-start | bytes 20480 | tf_op jit(solution)/shard_map/reduce_scatter | solution.py:50
  6.5 7.9 %collective-permute-start = (f32[8,128]{1,0:T(8,128)}, f32[8,128]{1,0:T(8,128)S(1)}, u32[]{:S(2)}, u32[]{:S(2)}) collective-permute-start(f32[8,128]{1,0:T(8,128)} %param.5), channel_id=1, source_target_pairs={{0,4},{4,8},{8,12},{12,16},{16,20},{20,24},{24,28},{28,0},{1,5},{5... | collective-permute-start | bytes 12296 | tf_op jit(solution)/shard_map/ppermute | solution.py:14
  12.8 14.2 %copy-start.2 = (s32[1,64]{1,0:T(1,128)S(1)}, s32[1,64]{1,0:T(1,128)}, u32[]{:S(2)}) copy-start(s32[1,64]{1,0:T(1,128)} %param.8) | copy-start | bytes 772
  14.4 6.3 %collective-permute-start.1 = (f32[8,128]{1,0:T(8,128)S(1)}, f32[8,128]{1,0:T(8,128)S(1)}, u32[]{:S(2)}, u32[]{:S(2)}) collective-permute-start(f32[8,128]{1,0:T(8,128)S(1)} %collective-permute-done), channel_id=1, source_target_pairs={{0,4},{4,8},{8,12},{12,16},{16,20},{20,24},{24,28},{28,0},{1,5},{5... | collective-permute-start | bytes 12296 | tf_op jit(solution)/shard_map/ppermute | solution.py:14
  20.7 6.3 %collective-permute-start.2 = (f32[8,128]{1,0:T(8,128)S(1)}, f32[8,128]{1,0:T(8,128)S(1)}, u32[]{:S(2)}, u32[]{:S(2)}) collective-permute-start(f32[8,128]{1,0:T(8,128)S(1)} %collective-permute-done.1), channel_id=1, source_target_pairs={{0,4},{4,8},{8,12},{12,16},{16,20},{20,24},{24,28},{28,0},{1,5},{5... | collective-permute-start | bytes 12296 | tf_op jit(solution)/shard_map/ppermute | solution.py:14
  23.9 32.7 %copy-start.1 = (s32[1,64]{1,0:T(1,128)S(1)}, s32[1,64]{1,0:T(1,128)}, u32[]{:S(2)}) copy-start(s32[1,64]{1,0:T(1,128)} %param.7) | copy-start | bytes 772
  27.0 6.3 %collective-permute-start.3 = (f32[8,128]{1,0:T(8,128)S(1)}, f32[8,128]{1,0:T(8,128)S(1)}, u32[]{:S(2)}, u32[]{:S(2)}) collective-permute-start(f32[8,128]{1,0:T(8,128)S(1)} %collective-permute-done.2), channel_id=1, source_target_pairs={{0,4},{4,8},{8,12},{12,16},{16,20},{20,24},{24,28},{28,0},{1,5},{5... | collective-permute-start | bytes 12296 | tf_op jit(solution)/shard_map/ppermute | solution.py:14
  33.3 6.3 %collective-permute-start.4 = (f32[8,128]{1,0:T(8,128)S(1)}, f32[8,128]{1,0:T(8,128)S(1)}, u32[]{:S(2)}, u32[]{:S(2)}) collective-permute-start(f32[8,128]{1,0:T(8,128)S(1)} %collective-permute-done.3), channel_id=1, source_target_pairs={{0,4},{4,8},{8,12},{12,16},{16,20},{20,24},{24,28},{28,0},{1,5},{5... | collective-permute-start | bytes 12296 | tf_op jit(solution)/shard_map/ppermute | solution.py:14
  39.6 6.3 %collective-permute-start.5 = (f32[8,128]{1,0:T(8,128)S(1)}, f32[8,128]{1,0:T(8,128)S(1)}, u32[]{:S(2)}, u32[]{:S(2)}) collective-permute-start(f32[8,128]{1,0:T(8,128)S(1)} %collective-permute-done.4), channel_id=1, source_target_pairs={{0,4},{4,8},{8,12},{12,16},{16,20},{20,24},{24,28},{28,0},{1,5},{5... | collective-permute-start | bytes 12296 | tf_op jit(solution)/shard_map/ppermute | solution.py:14
  45.9 6.3 %collective-permute-start.6 = (f32[8,128]{1,0:T(8,128)S(1)}, f32[8,128]{1,0:T(8,128)S(1)}, u32[]{:S(2)}, u32[]{:S(2)}) collective-permute-start(f32[8,128]{1,0:T(8,128)S(1)} %collective-permute-done.5), channel_id=1, source_target_pairs={{0,4},{4,8},{8,12},{12,16},{16,20},{20,24},{24,28},{28,0},{1,5},{5... | collective-permute-start | bytes 12296 | tf_op jit(solution)/shard_map/ppermute | solution.py:14
  57.5 75.0 %reduce-scatter.5.cloned.1.call-start = ((), (), s32[]{:S(2)}) async-start(), calls=%async_computation.3 | async-start | bytes 36864 | tf_op jit(solution)/shard_map/reduce_scatter | solution.py:54
Sparse Core Ops, SparseCore 0:
  57.7 16.9 reduce-scatter.2
  77.8 54.6 reduce-scatter.4
